TPU v7x, 128 devices: a whole 4x4x4 slice. The times are simulated.
128 devices in a mesh: req: 16 (over y, z), head: 8 (over x, core).
Axes of the slice: x: 4, y: 4, z: 4, core: 2. Of those that a mesh axis runs over, the one named last changes fastest.
Arguments:
- hidden: bfloat16 [2048, 6144], P('req'), may hold values from -15 to 15
- attn_norm_gain: float32 [6144], replicated, may hold values from 0.3 to 3
- attn_norm_bias: float32 [6144], replicated, may hold values from -4 to 4
- mlp_norm_gain: float32 [6144], replicated, may hold values from 0.3 to 3
- mlp_norm_bias: float32 [6144], replicated, may hold values from -4 to 4
- qkv_weight: bfloat16 [6144, 9216], P('req', 'head'), may hold values from -0.078125 to 0.078125
- qkv_bias: float32 [9216], P('head'), may hold values from -3 to 3
- out_weight: bfloat16 [3072, 6144], P('head', 'req'), may hold values from -0.625 to 0.625
- out_bias: float32 [6144], replicated, may hold values from -3 to 3
- up_weight: bfloat16 [6144, 12288], P('req', 'head'), may hold values from -0.078125 to 0.078125
- up_bias: float32 [12288], P('head'), may hold values from -3 to 3
- down_weight: bfloat16 [12288, 6144], P('head', 'req'), may hold values from -0.0546875 to 0.0546875
- down_bias: float32 [6144], replicated, may hold values from -3 to 3
- cache_keys: bfloat16 [16, 4096, 3072], P('req', None, 'head'), may hold values from -1300 to 1300
- cache_values: bfloat16 [16, 4096, 3072], P('req', None, 'head'), may hold values from -6 to 6
- cached_len: int32 [16], P('req'), may hold values from 128 to 4096, as said below
Outputs:
- hidden_out: bfloat16 [2048, 6144], P('req')
- new_keys: bfloat16 [16, 128, 3072], P('req', None, 'head')
- new_values: bfloat16 [16, 128, 3072], P('req', None, 'head')
Inputs may be any that keep to these rules, and one draw needn't show every extreme that they name: `cached_len`: each entry is 128 or 4096, and both values occur.
All inputs are finite; a program needn't handle non-finite values.
Results may differ from a plain program's by a relative error of at most 0.0085.
The roundings to bfloat16 on the way count: a program that leaves them out, or rounds other values in their place, can miss the bound.
Values may be sent and summed in bfloat16 or wider, within the bound.
A program may use at most 128 MiB of HBM per device.

v0:
```python
import math
import jax
import jax.numpy as jnp
from jax import lax
from jax.sharding import PartitionSpec as P

DH = 96
ROT = 24
NEW = 128
CACHE = 4096
KBLOCK = 512


def normalize(values, norm_gain, norm_shift):
    widened = values.astype(jnp.float32)
    center = jnp.mean(widened, axis=-1, keepdims=True)
    spread = jnp.mean(jnp.square(widened - center), axis=-1, keepdims=True)
    return ((widened - center) * lax.rsqrt(spread + 1e-05) * norm_gain + norm_shift).astype(
        jnp.bfloat16
    )


def rotate(values, position):
    halfway = ROT // 2
    exponent = jnp.arange(halfway, dtype=jnp.float32) * (2.0 / ROT)
    frequency = jnp.power(10000.0, -exponent)
    angle = position[:, None] * frequency[None, :]
    cosine = jnp.cos(angle)[:, None, :]
    sine_part = jnp.sin(angle)[:, None, :]
    lower_half = values[..., :halfway]
    upper_half = values[..., halfway:ROT]
    return jnp.concatenate(
        [
            lower_half * cosine - upper_half * sine_part,
            upper_half * cosine + lower_half * sine_part,
            values[..., ROT:],
        ],
        axis=-1,
    )


def attend_request(qkv_rows, keys_old, values_old, length, local_heads):
    scale_factor = 1.0 / math.sqrt(DH)
    split_rows = qkv_rows.reshape(NEW, local_heads, 3, DH)
    position = length.astype(jnp.float32) + jnp.arange(NEW, dtype=jnp.float32)
    queries = rotate(split_rows[:, :, 0], position).astype(jnp.bfloat16)
    key_new = rotate(split_rows[:, :, 1], position).astype(jnp.bfloat16)
    value_new = split_rows[:, :, 2].astype(jnp.bfloat16)
    query_index = jnp.arange(NEW, dtype=jnp.int32)
    fresh_scores = (
        jnp.einsum("qhd,khd->hqk", queries, key_new, preferred_element_type=jnp.float32)
        * scale_factor
    )
    fresh_scores = jnp.where(
        (query_index[None, :] <= query_index[:, None])[None], fresh_scores, -1e30
    )
    block_total = (length + KBLOCK - 1) // KBLOCK
    key_offsets = jnp.arange(KBLOCK, dtype=jnp.int32)

    def score_block(block_index, carry):
        score_store, highest = carry
        first_key = block_index * KBLOCK
        key_block = lax.dynamic_slice_in_dim(keys_old, first_key, KBLOCK, 0)
        block_scores = (
            jnp.einsum("qhd,khd->hqk", queries, key_block, preferred_element_type=jnp.float32)
            * scale_factor
        )
        block_scores = jnp.where(
            (first_key + key_offsets < length)[None, None, :], block_scores, -1e30
        )
        score_store = lax.dynamic_update_slice_in_dim(score_store, block_scores, first_key, 2)
        return (score_store, jnp.maximum(highest, jnp.max(block_scores, axis=-1)))

    empty_store = jnp.zeros((local_heads, NEW, CACHE), jnp.float32)
    score_store, highest = lax.fori_loop(
        0, block_total, score_block, (empty_store, jnp.max(fresh_scores, axis=-1))
    )
    fresh_weights = jnp.exp(fresh_scores - highest[..., None])

    def weigh_block(block_index, carry):
        mixed, denominator = carry
        first_key = block_index * KBLOCK
        block_scores = lax.dynamic_slice_in_dim(score_store, first_key, KBLOCK, 2)
        block_weights = jnp.exp(block_scores - highest[..., None])
        value_block = lax.dynamic_slice_in_dim(values_old, first_key, KBLOCK, 0)
        mixed = mixed + jnp.einsum(
            "hqk,khd->qhd",
            block_weights.astype(jnp.bfloat16),
            value_block,
            preferred_element_type=jnp.float32,
        )
        return (mixed, denominator + jnp.sum(block_weights, axis=-1))

    initial = (
        jnp.einsum(
            "hqk,khd->qhd",
            fresh_weights.astype(jnp.bfloat16),
            value_new,
            preferred_element_type=jnp.float32,
        ),
        jnp.sum(fresh_weights, axis=-1),
    )
    mixed, denominator = lax.fori_loop(0, block_total, weigh_block, initial)
    attended = (mixed / jnp.transpose(denominator)[:, :, None]).astype(jnp.bfloat16)
    width = local_heads * DH
    return (
        attended.reshape(NEW, width),
        key_new.reshape(NEW, width),
        value_new.reshape(NEW, width),
    )


def body(
    hidden,
    attn_norm_gain,
    attn_norm_bias,
    mlp_norm_gain,
    mlp_norm_bias,
    qkv_weight,
    qkv_bias,
    out_weight,
    out_bias,
    up_weight,
    up_bias,
    down_weight,
    down_bias,
    cache_keys,
    cache_values,
    cached_len,
):
    qkv_cols = qkv_weight.shape[1]
    local_heads = qkv_cols // (3 * DH)
    attn_normed = normalize(hidden, attn_norm_gain, attn_norm_bias)
    mlp_normed = normalize(hidden, mlp_norm_gain, mlp_norm_bias)
    attn_blocks, mlp_blocks = (
        lax.all_to_all(attn_normed, "req", split_axis=1, concat_axis=0, tiled=True),
        lax.all_to_all(mlp_normed, "req", split_axis=1, concat_axis=0, tiled=True),
    )
    qkv_term = jnp.dot(attn_blocks, qkv_weight, preferred_element_type=jnp.float32)
    up_term = jnp.dot(mlp_blocks, up_weight, preferred_element_type=jnp.float32)
    summed = lax.psum_scatter(
        jnp.concatenate([qkv_term, up_term], axis=1), "req", scatter_dimension=0, tiled=True
    )
    qkv_sum = summed[:, :qkv_cols]
    up_sum = summed[:, qkv_cols:]
    qkv = qkv_sum + qkv_bias
    units = jax.nn.gelu(up_sum + up_bias, approximate=True).astype(jnp.bfloat16)
    keys_old = cache_keys[0].reshape(CACHE, local_heads, DH)
    values_old = cache_values[0].reshape(CACHE, local_heads, DH)
    attended_rows, key_rows, value_rows = attend_request(
        qkv, keys_old, values_old, cached_len[0], local_heads
    )
    key_list = [key_rows]
    value_list = [value_rows]
    new_keys = jnp.stack(key_list, axis=0)
    new_values = jnp.stack(value_list, axis=0)
    joined = jnp.concatenate([attended_rows, units], axis=1)
    head_width = attended_rows.shape[1]
    shard_rows = lax.all_gather(joined, "req", axis=0, tiled=True)
    attention_part = jnp.dot(
        shard_rows[:, :head_width], out_weight, preferred_element_type=jnp.float32
    )
    partial_out = attention_part + jnp.dot(
        shard_rows[:, head_width:], down_weight, preferred_element_type=jnp.float32
    )
    bias_total = out_bias + down_bias
    spread_out = lax.all_to_all(partial_out, "req", split_axis=0, concat_axis=1, tiled=True)
    summed_out = lax.psum(spread_out, "head")
    result = (hidden.astype(jnp.float32) + summed_out + bias_total).astype(jnp.bfloat16)
    return (result, new_keys, new_values)


def solution(mesh):
    return jax.shard_map(
        body,
        mesh=mesh,
        in_specs=(
            P("req", None),
            P(),
            P(),
            P(),
            P(),
            P("req", "head"),
            P("head"),
            P("head", "req"),
            P(),
            P("req", "head"),
            P("head"),
            P("head", "req"),
            P(),
            P("req", None, "head"),
            P("req", None, "head"),
            P("req"),
        ),
        out_specs=(P("req", None), P("req", None, "head"), P("req", None, "head")),
        check_vma=False,
    )
```

profile of v0, /device:TPU:0, one launch (start us, length us, event | category | flops | bytes accessed | tf_op | source)
XLA Modules:
  0.0 498.3 jit_solution(11655447223252928488)
XLA Ops:
  7.2 2.0 copy.39
  9.2 0.8 convert_reduce_fusion
  10.1 0.8 fusion.24
  10.9 5.4 %fusion.21 = (bf16[128,6144]{0,1:T(8,128)(2,1)}, bf16[128,6144]{0,1:T(8,128)(2,1)S(1)}) fusion(bf16[128,6144]{0,1:T(8,128)(2,1)S(1)} %copy.39, f32[6144]{0:T(1024)S(1)} %copy-done.7, f32[6144]{0:T(1024)S(1)} %copy-done.8, f32[128]{0:T(128)S(1)} %add_rsqrt_fusion, f32[128]{0:T(128)S(1)} %broadcast_multiply_fusion, f32[6144]{0:T(1024)S(1)} %copy-done.9, ...), kind=kLoop, calls=%fused_computation.29 | loop fusion | flops 7077888 | bytes 4817920 | tf_op jit(solution)/shard_map/convert_element_type | solution.py:18
  16.4 30.6 %all_to_all.57 = bf16[128,16,384]{0,2,1:T(8,128)(2,1)} all-to-all(bf16[128,16,384]{0,2,1:T(8,128)(2,1)S(1)} %bitcast.67), channel_id=1, replica_groups=mesh['req'=16,'head'=8] {'req'}, dimensions={1} | all-to-all | bytes 3145728 | tf_op jit(solution)/shard_map/all_to_all | solution.py:137
  47.0 3.8 all-to-all-start
  50.9 0.0 reduce-scatter.2.cloned.1.call-start
  50.9 2.6 copy.41
  53.5 19.9 %all-to-all-done = bf16[128,16,384]{0,2,1:T(8,128)(2,1)S(1)} async-done(((bf16[128,16,384]{0,2,1:T(8,128)(2,1)}), bf16[128,16,384]{0,2,1:T(8,128)(2,1)S(1)}, u32[]{:S(2)}, u32[]{:S(2)}) %all-to-all-start) | async-done | bytes 1572896 | tf_op jit(solution)/shard_map/all_to_all | solution.py:136
  73.4 1.1 copy-done.4
  74.6 1.9 copy.40
  76.5 5.1 %fusion.47 = f32[2048,1536]{0,1:T(8,128)S(1)} fusion(bf16[2048,384]{1,0:T(8,128)(2,1)} %bitcast.63, bf16[384,1536]{1,0:T(8,128)(2,1)S(1)} %copy-done), kind=kOutput, calls=%fused_computation.79 | convolution fusion | flops 2415919104 | bytes 15335424 | tf_op jit(solution)/shard_map/dot_general | solution.py:140
  81.6 2.8 fusion.46
  84.3 11.1 %pad_maximum_fusion = f32[2048,2688]{0,1:T(8,128)} fusion(f32[2048,1536]{0,1:T(8,128)S(1)} %fusion.47, f32[2048,1152]{0,1:T(8,128)S(1)} %fusion.46), kind=kLoop, calls=%fused_computation.18 | loop fusion | flops 5505024 | bytes 44040192 | tf_op jit(solution)/shard_map/concatenate | solution.py:142
  95.5 0.2 all-gather.2.cloned.1.call-start
  96.4 4.8 copy.45
  101.1 4.9 copy.47
  106.1 0.1 multiply_cosine_fusion
  106.2 124.0 %reduce-scatter.2.cloned.1.call-done = f32[128,2688]{0,1:T(8,128)} async-done(((f32[2048,2688]{0,1:T(8,128)}), f32[128,2688]{0,1:T(8,128)}) %reduce-scatter.2.cloned.1.call-update) | async-done | bytes 1376272 | tf_op jit(solution)/shard_map/reduce_scatter | solution.py:141
  230.3 1.3 slice_add_fusion.1
  231.7 0.3 fusion.44
  232.0 3.8 broadcast_in_dim.20
  235.7 3.0 while.26
  235.7 0.7 fusion.69
  236.4 2.4 fusion.70
  238.7 0.1 fusion.37
  238.8 0.2 convolution_bitcast_fusion.1
  239.0 3.4 while.25
  239.0 1.3 constant_dynamic-slice_fusion.2
  240.3 0.3 copy.59
  240.7 1.4 fusion.66
  242.1 0.3 fusion.67
  242.5 1.5 fusion.36
  244.0 0.8 pad_maximum_fusion.1
  244.8 0.0 all-gather.2.cloned.1.call-update
  244.8 0.0 all-reduce.2.cloned.1.call-start
  244.9 118.5 %all-gather.2.cloned.1.call-done = bf16[2048,1920]{0,1:T(8,128)(2,1)} async-done(((bf16[128,1920]{0,1:T(8,128)(2,1)}), bf16[2048,1920]{0,1:T(8,128)(2,1)}) %all-gather.2.cloned.1.call-update) | async-done | bytes 7864336 | tf_op jit(solution)/shard_map/all_gather | solution.py:159
  363.4 5.9 %fusion.14 = f32[2048,384]{1,0:T(8,128)S(1)} fusion(bf16[1536,384]{1,0:T(8,128)(2,1)} %param.31, bf16[2048,1920]{0,1:T(8,128)(2,1)} %all-gather.2.cloned.1.call-done), kind=kOutput, calls=%fused_computation.19 | convolution fusion | flops 2415919104 | bytes 10616832 | tf_op jit(solution)/shard_map/dot_general | solution.py:163
  369.3 2.6 convolution_add_fusion
  371.9 42.9 %all_to_all.58 = f32[16,128,384]{2,1,0:T(8,128)} all-to-all(f32[16,128,384]{2,1,0:T(8,128)S(1)} %bitcast.60), channel_id=1, replica_groups=mesh['req'=16,'head'=8] {'req'}, dimensions={0} | all-to-all | bytes 6291456 | tf_op jit(solution)/shard_map/all_to_all | solution.py:167
  414.9 3.6 copy.49
  418.4 0.7 copy-done.11
  419.1 0.0 copy-done.12
  419.2 0.8 copy.51
  419.9 0.8 copy.52
  420.7 65.2 %all-reduce.2.cloned.1.call-done = f32[128,6144]{0,1:T(8,128)} async-done(((f32[128,6144]{0,1:T(8,128)}), f32[128,6144]{0,1:T(8,128)}) %all-reduce.2.cloned.1.call-update) | async-done | bytes 3145744 | tf_op jit(solution)/shard_map/psum | solution.py:168
  485.9 3.3 fusion.26
  489.2 2.6 copy.50
  (45 shorter events, 0.3 us)
Async XLA Ops:
  7.2 69.3 %copy-start = (bf16[384,1536]{1,0:T(8,128)(2,1)S(1)}, bf16[384,1536]{1,0:T(8,128)(2,1)}, u32[]{:S(2)}) copy-start(bf16[384,1536]{1,0:T(8,128)(2,1)} %param.29) | copy-start | bytes 3538948
  7.2 3.7 copy-start.8
  7.2 3.7 copy-start.7
  7.2 3.7 copy-start.10
  7.2 3.7 copy-start.9
  9.2 7.2 %copy-start.2 = (bf16[128,6144]{0,1:T(8,128)(2,1)}, bf16[128,6144]{0,1:T(8,128)(2,1)S(1)}, u32[]{:S(2)}) copy-start(bf16[128,6144]{0,1:T(8,128)(2,1)S(1)} %copy.39) | copy-start | bytes 4718596
  47.0 26.4 %all-to-all-start = ((bf16[128,16,384]{0,2,1:T(8,128)(2,1)}), bf16[128,16,384]{0,2,1:T(8,128)(2,1)S(1)}, u32[]{:S(2)}, u32[]{:S(2)}) async-start(bf16[128,16,384]{0,2,1:T(8,128)(2,1)} %bitcast.66), calls=%async_computation | async-start | bytes 3145728 | tf_op jit(solution)/shard_map/all_to_all | solution.py:136
  50.9 179.4 %reduce-scatter.2.cloned.1.call-start = ((), (), s32[]{:S(2)}) async-start(), calls=%async_computation.4 | async-start | bytes 23396352 | tf_op jit(solution)/shard_map/reduce_scatter | solution.py:141
  73.4 1.1 copy-start.4
  76.4 5.1 %copy-start.5 = (bf16[384,1152]{1,0:T(8,128)(2,1)S(1)}, bf16[384,1152]{1,0:T(8,128)(2,1)}, u32[]{:S(2)}) copy-start(bf16[384,1152]{1,0:T(8,128)(2,1)} %param.25) | copy-start | bytes 2654212
  95.5 267.9 %all-gather.2.cloned.1.call-start = ((), (), s32[]{:S(2)}) async-start(), calls=%async_computation.5 | async-start | bytes 8355840 | tf_op jit(solution)/shard_map/all_gather | solution.py:159
  101.1 129.1 %copy-start.13 = (f32[1152]{0:T(1024)S(1)}, f32[1152]{0:T(1024)}, u32[]{:S(2)}) copy-start(f32[1152]{0:T(1024)} %param.26) | copy-start | bytes 13828
  239.0 3.5 copy-start.14
  244.8 124.5 %copy-start.6 = (bf16[384,384]{1,0:T(8,128)(2,1)S(1)}, bf16[384,384]{1,0:T(8,128)(2,1)}, u32[]{:S(2)}) copy-start(bf16[384,384]{1,0:T(8,128)(2,1)} %param.27) | copy-start | bytes 884740
  244.8 241.0 %all-reduce.2.cloned.1.call-start = ((), (), s32[]{:S(2)}) async-start(), calls=%async_computation.6 | async-start | bytes 6291456 | tf_op jit(solution)/shard_map/psum | solution.py:168
  418.4 0.7 copy-start.11
  418.4 0.8 copy-start.12
  418.4 67.5 %copy-start.3 = (bf16[128,6144]{0,1:T(8,128)(2,1)S(1)}, bf16[128,6144]{0,1:T(8,128)(2,1)}, u32[]{:S(2)}) copy-start(bf16[128,6144]{0,1:T(8,128)(2,1)} %copy-done.2) | copy-start | bytes 4718596
  485.9 5.9 %copy-start.1 = (bf16[384,1536]{1,0:T(8,128)(2,1)S(1)}, bf16[384,1536]{1,0:T(8,128)(2,1)}, u32[]{:S(2)}) copy-start(bf16[384,1536]{1,0:T(8,128)(2,1)} %param.29) | copy-start | bytes 3538948
Sparse Core Ops, SparseCore 0:
  95.6 134.6 reduce-scatter.1
  244.9 118.4 all-gather.1
  418.6 67.2 all-reduce.1
where the time goes:
time: 500 us; the launch traced here: 498 us
  waiting for transfers between devices  328 us (66%)
  blocking collectives  73.5 us (15%)
  local copies, waits for them, and re-layouts  31.2 us (6%)
  other arithmetic  26.5 us (5%)
  matrix products  20.5 us (4%)
  between operations  14.7 us (3%)
    reduce_scatter x1, waiting for transfers between devices, body(): lax.psum_scatter(jnp.concatenate([qkv_term, up_term], axis=1), 'req', sca...  124 us
    all_gather x1, waiting for transfers between devices, body(): shard_rows = lax.all_gather(joined, 'req', axis=0, tiled=True)  119 us
    psum x1, waiting for transfers between devices, body(): summed_out = lax.psum(spread_out, 'head')  65.2 us
    all_to_all x1, blocking collectives, body(): lax.all_to_all(partial_out, 'req', split_axis=0, concat_axis=1, tiled=True)  42.9 us
    all_to_all x1, blocking collectives, body(): lax.all_to_all(mlp_normed, 'req', split_axis=1, concat_axis=0, tiled=True)  30.6 us
    all_to_all x1, waiting for transfers between devices, body(): lax.all_to_all(attn_normed, 'req', split_axis=1, concat_axis=0, tiled=True)  19.9 us
    unnamed x36, local copies, waits for them, and re-layouts  17.7 us
    concatenate x1, other arithmetic, body(): jnp.concatenate([qkv_term, up_term], axis=1)  11.1 us
  transfers between devices with their start and end apart: 4, of which 4 were waited for; matrix products, arithmetic and copies ran while one was open for 3% of the time, Pallas kernels for 0%

commit v1 on v0

--- a/solution.py
+++ b/solution.py
@@ -156,7 +156,8 @@
     new_values = jnp.stack(value_list, axis=0)
     joined = jnp.concatenate([attended_rows, units], axis=1)
     head_width = attended_rows.shape[1]
-    shard_rows = lax.all_gather(joined, "req", axis=0, tiled=True)
+    sent = jnp.stack([joined] * lax.axis_size("req"))
+    shard_rows = jnp.concatenate(lax.all_to_all(sent, "req", 0, 0), axis=0)
     attention_part = jnp.dot(
         shard_rows[:, :head_width], out_weight, preferred_element_type=jnp.float32
     )

time: 500 us -> 518 us (1.036)
  blocking collectives: 73.5 us -> 213 us
  waiting for transfers between devices: 328 us -> 209 us
    all_to_all x0 -> x1, blocking collectives: none -> 140 us  [body(): shard_rows = jnp.concatenate(lax.all_to_all(sent, 'req', 0, 0), axis=0)]
    all_gather x1 -> x0, waiting for transfers between devices: 119 us -> none  [body(): shard_rows = lax.all_gather(joined, 'req', axis=0, tiled=True)]
    unnamed x36 -> x38, local copies, waits for them, and re-layouts: 17.7 us -> 17.6 us
  transfers between devices with their start and end apart: 4 -> 3, of which waited for: 4 -> 3; matrix products, arithmetic and copies ran while one was open for 3% -> 3% of each run, Pallas kernels for 0% -> 0%
where the time goes in v1:
time: 518 us; the launch traced here: 516 us
  blocking collectives  213 us (41%)
  waiting for transfers between devices  209 us (40%)
  local copies, waits for them, and re-layouts  32.4 us (6%)
  other arithmetic  25.7 us (5%)
  matrix products  16.6 us (3%)
  between operations  15 us (3%)
    all_to_all x1, blocking collectives, body(): shard_rows = jnp.concatenate(lax.all_to_all(sent, 'req', 0, 0), axis=0)  140 us
    reduce_scatter x1, waiting for transfers between devices, body(): lax.psum_scatter(jnp.concatenate([qkv_term, up_term], axis=1), 'req', sca...  124 us
    psum x1, waiting for transfers between devices, body(): summed_out = lax.psum(spread_out, 'head')  65 us
    all_to_all x1, blocking collectives, body(): lax.all_to_all(partial_out, 'req', split_axis=0, concat_axis=1, tiled=True)  42.5 us
    all_to_all x1, blocking collectives, body(): lax.all_to_all(mlp_normed, 'req', split_axis=1, concat_axis=0, tiled=True)  30.6 us
    all_to_all x1, waiting for transfers between devices, body(): lax.all_to_all(attn_normed, 'req', split_axis=1, concat_axis=0, tiled=True)  19.9 us
    unnamed x38, local copies, waits for them, and re-layouts  17.6 us
    concatenate x1, other arithmetic, body(): jnp.concatenate([qkv_term, up_term], axis=1)  11.1 us
  transfers between devices with their start and end apart: 3, of which 3 were waited for; matrix products, arithmetic and copies ran while one was open for 3% of the time, Pallas kernels for 0%

profile of v1, /device:TPU:0, one launch (start us, length us, event | category | flops | bytes accessed | tf_op | source)
XLA Modules:
  0.0 515.9 jit_solution(6979880170638114271)
XLA Ops:
  7.2 2.0 copy.41
  9.2 0.8 convert_reduce_fusion
  10.1 0.8 fusion.24
  10.9 5.4 %fusion.21 = (bf16[128,6144]{0,1:T(8,128)(2,1)}, bf16[128,6144]{0,1:T(8,128)(2,1)S(1)}) fusion(bf16[128,6144]{0,1:T(8,128)(2,1)S(1)} %copy.41, f32[6144]{0:T(1024)S(1)} %copy-done.7, f32[6144]{0:T(1024)S(1)} %copy-done.8, f32[128]{0:T(128)S(1)} %add_rsqrt_fusion, f32[128]{0:T(128)S(1)} %broadcast_multiply_fusion, f32[6144]{0:T(1024)S(1)} %copy-done.9, ...), kind=kLoop, calls=%fused_computation.29 | loop fusion | flops 7077888 | bytes 4817920 | tf_op jit(solution)/shard_map/convert_element_type | solution.py:18
  16.4 30.6 %all_to_all.62 = bf16[128,16,384]{0,2,1:T(8,128)(2,1)} all-to-all(bf16[128,16,384]{0,2,1:T(8,128)(2,1)S(1)} %bitcast.70), channel_id=1, replica_groups=mesh['req'=16,'head'=8] {'req'}, dimensions={1} | all-to-all | bytes 3145728 | tf_op jit(solution)/shard_map/all_to_all | solution.py:137
  47.0 3.8 all-to-all-start
  50.9 0.0 reduce-scatter.2.cloned.1.call-start
  50.9 2.6 copy.43
  53.5 19.9 %all-to-all-done = bf16[128,16,384]{0,2,1:T(8,128)(2,1)S(1)} async-done(((bf16[128,16,384]{0,2,1:T(8,128)(2,1)}), bf16[128,16,384]{0,2,1:T(8,128)(2,1)S(1)}, u32[]{:S(2)}, u32[]{:S(2)}) %all-to-all-start) | async-done | bytes 1572896 | tf_op jit(solution)/shard_map/all_to_all | solution.py:136
  73.4 1.1 copy-done.4
  74.6 1.9 copy.42
  76.5 5.1 fusion.47
  81.6 2.8 fusion.46
  84.3 11.1 %pad_maximum_fusion = f32[2048,2688]{0,1:T(8,128)} fusion(f32[2048,1536]{0,1:T(8,128)S(1)} %fusion.47, f32[2048,1152]{0,1:T(8,128)S(1)} %fusion.46), kind=kLoop, calls=%fused_computation.18 | loop fusion | flops 5505024 | bytes 44040192 | tf_op jit(solution)/shard_map/concatenate | solution.py:142
  95.4 0.0 reduce-scatter.2.cloned.1.call-update
  95.4 0.2 all-reduce.2.cloned.1.call-start
  96.3 4.7 copy.47
  101.1 4.9 copy.49
  106.0 0.1 multiply_cosine_fusion
  106.1 124.1 %reduce-scatter.2.cloned.1.call-done = f32[128,2688]{0,1:T(8,128)} async-done(((f32[2048,2688]{0,1:T(8,128)}), f32[128,2688]{0,1:T(8,128)}) %reduce-scatter.2.cloned.1.call-update) | async-done | bytes 1376272 | tf_op jit(solution)/shard_map/reduce_scatter | solution.py:141
  230.2 1.3 slice_add_fusion.1
  231.7 0.3 fusion.44
  231.9 3.8 broadcast_in_dim.20
  235.7 3.0 while.26
  235.7 0.7 fusion.69
  236.4 2.4 fusion.70
  238.7 0.1 fusion.37
  238.8 0.2 convolution_bitcast_fusion.1
  239.0 3.4 while.25
  239.0 1.3 constant_dynamic-slice_fusion.2
  240.3 0.3 copy.62
  240.7 1.4 fusion.66
  242.0 0.3 fusion.67
  242.5 1.5 fusion.36
  244.0 0.3 copy.51
  244.3 1.0 stack.2
  245.3 139.9 %all_to_all.63 = bf16[16,128,1920]{2,1,0:T(8,128)(2,1)S(1)} all-to-all(bf16[16,128,1920]{2,1,0:T(8,128)(2,1)S(1)} %stack.2), channel_id=1, replica_groups=mesh['req'=16,'head'=8] {'req'}, dimensions={0} | all-to-all | bytes 15728640 | tf_op jit(solution)/shard_map/all_to_all | solution.py:160
  385.2 3.4 fusion.14
  388.6 1.2 convolution_add_fusion
  389.8 42.5 %all_to_all.64 = f32[16,128,384]{2,1,0:T(8,128)} all-to-all(f32[16,128,384]{2,1,0:T(8,128)S(1)} %bitcast.61), channel_id=1, replica_groups=mesh['req'=16,'head'=8] {'req'}, dimensions={0} | all-to-all | bytes 6291456 | tf_op jit(solution)/shard_map/all_to_all | solution.py:168
  432.3 3.6 copy.52
  435.9 0.7 copy-done.11
  436.6 0.0 copy-done.12
  436.6 0.8 copy.54
  437.4 0.8 copy.55
  438.2 65.0 %all-reduce.2.cloned.1.call-done = f32[128,6144]{0,1:T(8,128)} async-done(((f32[128,6144]{0,1:T(8,128)}), f32[128,6144]{0,1:T(8,128)}) %all-reduce.2.cloned.1.call-update) | async-done | bytes 3145744 | tf_op jit(solution)/shard_map/psum | solution.py:169
  503.1 3.4 fusion.26
  506.5 2.6 copy.53
  (47 shorter events, 0.4 us)
Async XLA Ops:
  7.2 69.3 %copy-start = (bf16[384,1536]{1,0:T(8,128)(2,1)S(1)}, bf16[384,1536]{1,0:T(8,128)(2,1)}, u32[]{:S(2)}) copy-start(bf16[384,1536]{1,0:T(8,128)(2,1)} %param.29) | copy-start | bytes 3538948
  7.2 3.7 copy-start.8
  7.2 3.7 copy-start.7
  7.2 3.7 copy-start.10
  7.2 3.7 copy-start.9
  9.2 7.2 %copy-start.2 = (bf16[128,6144]{0,1:T(8,128)(2,1)}, bf16[128,6144]{0,1:T(8,128)(2,1)S(1)}, u32[]{:S(2)}) copy-start(bf16[128,6144]{0,1:T(8,128)(2,1)S(1)} %copy.41) | copy-start | bytes 4718596
  47.0 26.4 %all-to-all-start = ((bf16[128,16,384]{0,2,1:T(8,128)(2,1)}), bf16[128,16,384]{0,2,1:T(8,128)(2,1)S(1)}, u32[]{:S(2)}, u32[]{:S(2)}) async-start(bf16[128,16,384]{0,2,1:T(8,128)(2,1)} %bitcast.69), calls=%async_computation | async-start | bytes 3145728 | tf_op jit(solution)/shard_map/all_to_all | solution.py:136
  50.9 179.4 %reduce-scatter.2.cloned.1.call-start = ((), (), s32[]{:S(2)}) async-start(), calls=%async_computation.5 | async-start | bytes 23396352 | tf_op jit(solution)/shard_map/reduce_scatter | solution.py:141
  73.4 1.1 copy-start.4
  76.4 5.1 copy-start.5
  95.4 407.7 %all-reduce.2.cloned.1.call-start = ((), (), s32[]{:S(2)}) async-start(), calls=%async_computation.6 | async-start | bytes 6291456 | tf_op jit(solution)/shard_map/psum | solution.py:169
  101.1 129.2 %copy-start.13 = (f32[1152]{0:T(1024)S(1)}, f32[1152]{0:T(1024)}, u32[]{:S(2)}) copy-start(f32[1152]{0:T(1024)} %param.26) | copy-start | bytes 13828
  239.0 3.5 copy-start.14
  245.3 139.9 %copy-start.15 = (bf16[1536,384]{1,0:T(8,128)(2,1)S(1)}, bf16[1536,384]{1,0:T(8,128)(2,1)}, u32[]{:S(2)}) copy-start(bf16[1536,384]{1,0:T(8,128)(2,1)} %param.31) | copy-start | bytes 3538948
  385.2 3.4 copy-start.6
  435.9 0.7 copy-start.11
  435.9 0.8 copy-start.12
  435.9 67.2 %copy-start.3 = (bf16[128,6144]{0,1:T(8,128)(2,1)S(1)}, bf16[128,6144]{0,1:T(8,128)(2,1)}, u32[]{:S(2)}) copy-start(bf16[128,6144]{0,1:T(8,128)(2,1)} %copy-done.2) | copy-start | bytes 4718596
  503.1 5.9 %copy-start.1 = (bf16[384,1536]{1,0:T(8,128)(2,1)S(1)}, bf16[384,1536]{1,0:T(8,128)(2,1)}, u32[]{:S(2)}) copy-start(bf16[384,1536]{1,0:T(8,128)(2,1)} %param.29) | copy-start | bytes 3538948
Sparse Core Ops, SparseCore 0:
  95.6 134.6 reduce-scatter.1
  436.0 67.0 all-reduce.1
